TPU v7x, 512 devices: a whole 4x4x16 slice. The times are simulated.
512 devices in a mesh: dom: 32 (over x_lo, z), grid: 16 (over x_hi, y, core).
Axes of the slice: x: 4 (x_hi: 2, x_lo: 2; x = x_hi * 2 + x_lo), y: 4, z: 16, core: 2. Of those that a mesh axis runs over, the one named last changes fastest.
Arguments:
- node_feats: bfloat16 [65536, 512], P(('dom', 'grid')), may hold values from -6 to 6
- adj_vals: bfloat16 [32, 16, 16, 4, 128, 128], P('dom', 'grid'), may hold values from -0.109375 to 0.109375
- adj_col: int32 [32, 16, 16, 4], P('dom', 'grid'), may hold values from 0 to 31
- adj_count: int32 [32, 16, 16], P('dom', 'grid'), may hold values from 0 to 4, as said below
- hist_store: bfloat16 [512, 16384], P('grid', 'dom'), may hold values from -6 to 6
- hist_list: int32 [32, 40], replicated, may hold values from 0 to 127, as said below
- hist_adj: bfloat16 [32, 40, 128, 128], P('dom'), may hold values from -0.3125 to 0.3125
- hist_row: int32 [32, 40], P('dom'), may hold values from 0 to 15
- hist_col: int32 [32, 40], P('dom'), may hold values from 0 to 39, each once within a row
- w_first: bfloat16 [512, 512], replicated, may hold values from -0.25 to 0.25
- w_second: bfloat16 [512, 512], replicated, may hold values from -0.25 to 0.25
Outputs:
- hidden: bfloat16 [65536, 512], P(('dom', 'grid'))
- embedding: bfloat16 [65536, 512], P(('dom', 'grid'))
Inputs may be any that keep to these rules, and one draw needn't show every extreme that they name: `adj_count`: slots of a block row at or beyond its count hold values that take no part. Some block row of some tile has 4 live slots. `hist_list`: the ids in one partition's list are distinct; at most 2 of them belong to one owner partition (owner = id // 4), and some list has 2 from one owner.
All inputs are finite; a program needn't handle non-finite values.
Results may differ from a plain program's by a relative error of at most 0.024.
Values may be sent and summed in bfloat16 or wider, within the bound.
No kernel may reach another device: no remote copies, remote signals or barrier semaphores. Data moves between devices by JAX's collectives and lax.ppermute only.
A program may use at most 64 MiB of HBM per device.

v0:
```python
import jax
import jax.numpy as jnp
from jax import lax
from jax.sharding import PartitionSpec as P

F = 512
BLOCK = 128
HOWN = 4
CAP = 2


def tile_product(col_panel, live_vals, tile_cols):
    blocks = col_panel.reshape(-1, BLOCK, col_panel.shape[1])
    picked = jnp.take(blocks, tile_cols, axis=0)
    summed = jnp.einsum("rkab,rkbf->raf", live_vals, picked, preferred_element_type=jnp.float32)
    return summed.reshape(-1, col_panel.shape[1])


def aggregate(source, live_vals, tile_cols, extra_term):
    col_panel = lax.all_gather(source, "dom", axis=0, tiled=True)
    partial_value = tile_product(col_panel, live_vals, tile_cols)
    if extra_term is not None:
        partial_value = partial_value + extra_term
    rounded = lax.optimization_barrier(partial_value.astype(jnp.bfloat16))
    return lax.psum_scatter(
        rounded.astype(jnp.float32).astype(jnp.bfloat16), "grid", scatter_dimension=0, tiled=True
    )


def history_term(hist_store, hist_list, local_adj, local_rows, local_cols, tile_rows):
    list_length = hist_list.shape[1]
    dom_index = lax.axis_index("dom")
    owner_ids = hist_list // HOWN
    local_ids = hist_list % HOWN
    same_owner = owner_ids[:, :, None] == owner_ids[:, None, :]
    earlier = jnp.arange(list_length)[None, :] < jnp.arange(list_length)[:, None]
    order_rank = jnp.sum(same_owner & earlier[None, :, :], axis=2)
    chosen_mask = (owner_ids == dom_index)[:, :, None, None]
    chosen_mask = chosen_mask & (
        order_rank[:, :, None, None] == jnp.arange(CAP)[None, None, :, None]
    )
    chosen_mask = chosen_mask & (
        local_ids[:, :, None, None] == jnp.arange(HOWN)[None, None, None, :]
    )
    selector = jnp.sum(chosen_mask.astype(jnp.int32), axis=1).astype(jnp.bfloat16)
    own_blocks = hist_store.reshape(hist_store.shape[0], HOWN, BLOCK)
    outgoing = jnp.einsum(
        "rch,fhb->rcfb", selector, own_blocks, preferred_element_type=jnp.float32
    ).astype(jnp.bfloat16)
    incoming = lax.all_to_all(outgoing, "dom", split_axis=0, concat_axis=0, tiled=True)
    flat_blocks = incoming.reshape(-1, incoming.shape[2], incoming.shape[3])
    mine_owner = lax.dynamic_index_in_dim(owner_ids, dom_index, 0, keepdims=False)
    mine_rank = lax.dynamic_index_in_dim(order_rank, dom_index, 0, keepdims=False)
    fetched = jnp.take(flat_blocks, mine_owner * CAP + mine_rank, axis=0)
    chosen = jnp.take(fetched, local_cols, axis=0)
    contribs = jnp.einsum("sfb,sab->sfa", chosen, local_adj, preferred_element_type=jnp.float32)
    row_onehot = (local_rows[None, :] == jnp.arange(tile_rows)[:, None]).astype(jnp.float32)
    summed = jnp.einsum("rs,sfa->rfa", row_onehot, contribs, precision=lax.Precision.HIGHEST)
    return summed.transpose(0, 2, 1).reshape(tile_rows * BLOCK, -1)


def local(
    node_feats,
    adj_vals,
    adj_col,
    adj_count,
    hist_store,
    hist_list,
    hist_adj,
    hist_row,
    hist_col,
    w_first,
    w_second,
):
    tile_vals = adj_vals[0, 0]
    tile_cols = adj_col[0, 0]
    row_counts = adj_count[0, 0]
    tile_rows = tile_vals.shape[0]
    live_mask = (jnp.arange(tile_vals.shape[1])[None, :] < row_counts[:, None]).astype(jnp.bfloat16)
    live_vals = tile_vals * live_mask[:, :, None, None]
    agg_first = aggregate(node_feats, live_vals, tile_cols, None)
    hidden = jax.nn.relu(jnp.dot(agg_first, w_first, preferred_element_type=jnp.float32)).astype(
        jnp.bfloat16
    )
    hist_part = history_term(
        hist_store, hist_list, hist_adj[0], hist_row[0], hist_col[0], tile_rows
    )
    grid_index = lax.axis_index("grid")
    placed = lax.dynamic_update_slice_in_dim(
        jnp.zeros((hist_part.shape[0], F), jnp.float32),
        hist_part,
        grid_index * hist_part.shape[1],
        1,
    )
    agg_second = aggregate(hidden, live_vals, tile_cols, placed)
    embedding = jnp.dot(agg_second, w_second, preferred_element_type=jnp.float32).astype(
        jnp.bfloat16
    )
    return (hidden, embedding)


def solution(mesh):
    placed = (
        P(("dom", "grid"), None),
        P("dom", "grid", None, None, None, None),
        P("dom", "grid", None, None),
        P("dom", "grid", None),
        P("grid", "dom"),
        P(),
        P("dom", None, None, None),
        P("dom", None),
        P("dom", None),
        P(),
        P(),
    )
    return jax.shard_map(
        local,
        mesh=mesh,
        in_specs=placed,
        out_specs=(P(("dom", "grid"), None), P(("dom", "grid"), None)),
        check_vma=False,
    )
```

profile of v0, /device:TPU:32, one launch (start us, length us, event | category | flops | bytes accessed | tf_op | source)
XLA Modules:
  0.0 524.1 jit_solution(14827638974284658832)
XLA Ops:
  7.2 0.0 copy-start
  7.2 0.0 all-gather.3.cloned.1.call-start
  7.2 0.7 all-gather.3.cloned.1.call-update
  7.9 0.0 reduce-scatter.3.cloned.1.call-start
  8.0 0.7 compare_select_fusion
  8.6 0.1 copy.32
  8.7 0.1 reshape.211
  8.8 0.7 compare_and_fusion
  9.5 0.1 copy.31
  9.6 0.7 fusion.22
  10.3 141.5 %all-gather.3.cloned.1.call-done = bf16[4096,512]{1,0:T(8,128)(2,1)} async-done(((bf16[128,512]{1,0:T(8,128)(2,1)}), bf16[4096,512]{1,0:T(8,128)(2,1)}) %all-gather.3.cloned.1.call-update) | async-done | bytes 4194320 | tf_op jit(solution)/shard_map/all_gather | solution.py:20
  151.8 7.7 %gather_fusion.2 = bf16[64,128,512]{2,1,0:T(8,128)(2,1)} fusion(bf16[32,128,512]{2,1,0:T(8,128)(2,1)} %bitcast.56, s32[1024]{0:T(1024)S(1)} %pad_clamp_fusion.2), kind=kCustom, calls=%fused_computation.clone | custom fusion | bytes 16777472 | tf_op jit(solution)/shard_map/jit(_take)/gather | solution.py:14
  159.5 0.0 copy-start.2
  159.5 0.0 copy-start.5
  159.5 0.0 copy-start.4
  159.5 7.2 %bitcast_convert_fusion = bf16[16,128,512]{2,1,0:T(8,128)(2,1)} fusion(bf16[16,4,128,512]{3,2,1,0:T(8,128)(2,1)} %bitcast.58, pred[16,4]{1,0:T(8,128)(4,1)S(1)} %copy.31, bf16[1,1,16,4,128,128]{5,4,3,2,1,0:T(8,128)(2,1)} %param.14, bf16[16,4]{1,0:T(8,128)(2,1)S(1)} %fusion.22), kind=kOutput, calls=%fused_computation.10 | convolution fusion | flops 1080033280 | bytes 12583104 | tf_op jit(solution)/shard_map/rkab,rkbf->raf/dot_general | solution.py:15
  166.7 0.0 copy-start.7
  166.7 0.0 reduce-scatter.3.cloned.1.call-update
  166.8 0.0 copy-start.6
  166.8 0.0 all-gather.5.cloned.1.call-start
  166.8 87.4 %reduce-scatter.3.cloned.1.call-done = bf16[128,512]{1,0:T(8,128)(2,1)} async-done(((bf16[2048,512]{1,0:T(8,128)(2,1)}), bf16[128,512]{1,0:T(8,128)(2,1)}) %reduce-scatter.3.cloned.1.call-update) | async-done | bytes 131088 | tf_op jit(solution)/shard_map/reduce_scatter | solution.py:25
  254.2 0.0 copy-done.2
  254.2 1.8 fusion.12
  256.0 0.0 all-gather.5.cloned.1.call-update
  256.1 0.0 copy-done.5
  256.1 0.0 copy-done.4
  256.2 0.8 convert_reduce_fusion
  257.0 0.2 convert_reduce_fusion.1
  257.3 0.3 convolution_convert_fusion
  257.6 1.0 copy.35
  258.6 13.0 %all-to-all-start = ((bf16[32,2,32,128]{3,2,1,0:T(8,128)(2,1)}), bf16[32,2,32,128]{3,2,1,0:T(8,128)(2,1)S(1)}, u32[]{:S(2)}, u32[]{:S(2)}) async-start(bf16[32,2,32,128]{3,2,1,0:T(8,128)(2,1)} %copy.35), calls=%async_computation.1 | async-start | bytes 1048576 | tf_op jit(solution)/shard_map/all_to_all | solution.py:50
  271.7 0.0 reduce-scatter.5.cloned.1.call-start
  271.7 0.0 copy-done.7
  271.8 36.6 %all-to-all-done = bf16[32,2,32,128]{3,2,1,0:T(8,128)(2,1)S(1)} async-done(((bf16[32,2,32,128]{3,2,1,0:T(8,128)(2,1)}), bf16[32,2,32,128]{3,2,1,0:T(8,128)(2,1)S(1)}, u32[]{:S(2)}, u32[]{:S(2)}) %all-to-all-start) | async-done | bytes 524320 | tf_op jit(solution)/shard_map/all_to_all | solution.py:50
  308.4 0.6 gather_fusion
  309.0 0.1 broadcast_select_fusion
  309.2 0.6 gather_fusion.1
  309.8 0.0 copy-done
  309.8 0.8 fusion.10
  310.6 0.0 copy-done.6
  310.6 0.7 convolution_bitcast_fusion
  311.3 0.3 copy.41
  311.7 91.9 %all-gather.5.cloned.1.call-done = bf16[4096,512]{1,0:T(8,128)(2,1)} async-done(((bf16[128,512]{1,0:T(8,128)(2,1)}), bf16[4096,512]{1,0:T(8,128)(2,1)}) %all-gather.5.cloned.1.call-update) | async-done | bytes 4194320 | tf_op jit(solution)/shard_map/all_gather | solution.py:20
  403.6 7.7 %gather_fusion.3 = bf16[64,128,512]{2,1,0:T(8,128)(2,1)} fusion(bf16[32,128,512]{2,1,0:T(8,128)(2,1)} %bitcast.55, s32[1024]{0:T(1024)S(1)} %pad_clamp_fusion.2), kind=kCustom, calls=%fused_computation.1.clone | custom fusion | bytes 16777472 | tf_op jit(solution)/shard_map/jit(_take)/gather | solution.py:14
  411.3 5.7 %fusion = f32[16,128,512,1]{2,1,3,0:T(8,128)S(1)} fusion(bf16[16,4,128,512]{3,2,1,0:T(8,128)(2,1)} %bitcast.57, pred[16,4]{1,0:T(8,128)(4,1)S(1)} %copy.31, bf16[1,1,16,4,128,128]{5,4,3,2,1,0:T(8,128)(2,1)} %param.14, bf16[16,4]{1,0:T(8,128)(2,1)S(1)} %fusion.22), kind=kOutput, calls=%fused_computation.4 | convolution fusion | flops 1078984704 | bytes 14680256 | tf_op jit(solution)/shard_map/rkab,rkbf->raf/dot_general | solution.py:15
  417.0 0.0 copy-start.1
  417.0 1.9 copy-done.1
  419.0 0.4 bitcast_add_fusion
  419.3 5.9 %add.103 = f32[2048,512]{1,0:T(8,128)} dynamic-update-slice(f32[2048,512]{1,0:T(8,128)} %bitcast.60, f32[2048,32]{1,0:T(8,128)S(1)} %bitcast_add_fusion, s32[]{:T(128)} %constant.76.clone.1, s32[]{:T(128)S(6)} %select_n.66) | dynamic-update-slice | bytes 524292 | tf_op jit(solution)/shard_map/add | solution.py:23
  425.2 0.0 copy-start.3
  425.2 3.8 convert_element_type.47
  429.1 0.0 reduce-scatter.5.cloned.1.call-update
  429.1 86.7 %reduce-scatter.5.cloned.1.call-done = bf16[128,512]{1,0:T(8,128)(2,1)} async-done(((bf16[2048,512]{1,0:T(8,128)(2,1)}), bf16[128,512]{1,0:T(8,128)(2,1)}) %reduce-scatter.5.cloned.1.call-update) | async-done | bytes 131088 | tf_op jit(solution)/shard_map/reduce_scatter | solution.py:25
  515.8 0.0 copy-done.3
  515.8 1.8 convolution_convert_fusion.1
  (12 shorter events, 0.1 us)
Async XLA Ops:
  7.2 302.6 %copy-start = (bf16[1,40,128,128]{3,2,1,0:T(8,128)(2,1)S(1)}, bf16[1,40,128,128]{3,2,1,0:T(8,128)(2,1)}, u32[]{:S(2)}) copy-start(bf16[1,40,128,128]{3,2,1,0:T(8,128)(2,1)} %param.19) | copy-start | bytes 3932164
  7.2 144.7 %all-gather.3.cloned.1.call-start = ((), (), s32[]{:S(2)}) async-start(), calls=%async_computation.3 | async-start | bytes 4325376 | tf_op jit(solution)/shard_map/all_gather | solution.py:20
  7.9 246.3 %reduce-scatter.3.cloned.1.call-start = ((), (), s32[]{:S(2)}) async-start(), calls=%async_computation.4 | async-start | bytes 2228224 | tf_op jit(solution)/shard_map/reduce_scatter | solution.py:25
  159.5 94.7 %copy-start.2 = (bf16[512,512]{1,0:T(8,128)(2,1)S(1)}, bf16[512,512]{1,0:T(8,128)(2,1)}, u32[]{:S(2)}) copy-start(bf16[512,512]{1,0:T(8,128)(2,1)} %param.22) | copy-start | bytes 1572868
  159.5 96.5 %copy-start.5 = (bf16[32,512]{1,0:T(8,128)(2,1)S(1)}, bf16[32,512]{1,0:T(8,128)(2,1)}, u32[]{:S(2)}) copy-start(bf16[32,512]{1,0:T(8,128)(2,1)} %param.17) | copy-start | bytes 98308
  159.5 96.6 %copy-start.4 = (s32[32,40]{1,0:T(8,128)S(1)}, s32[32,40]{1,0:T(8,128)}, u32[]{:S(2)}) copy-start(s32[32,40]{1,0:T(8,128)} %param.18) | copy-start | bytes 15364
  166.7 105.0 %copy-start.7 = (s32[1,40]{1,0:T(1,128)S(1)}, s32[1,40]{1,0:T(1,128)}, u32[]{:S(2)}) copy-start(s32[1,40]{1,0:T(1,128)} %param.21) | copy-start | bytes 484
  166.8 143.9 %copy-start.6 = (s32[1,40]{1,0:T(1,128)S(1)}, s32[1,40]{1,0:T(1,128)}, u32[]{:S(2)}) copy-start(s32[1,40]{1,0:T(1,128)} %param.20) | copy-start | bytes 484
  166.8 236.8 %all-gather.5.cloned.1.call-start = ((), (), s32[]{:S(2)}) async-start(), calls=%async_computation.5 | async-start | bytes 4325376 | tf_op jit(solution)/shard_map/all_gather | solution.py:20
  258.6 49.8 %all-to-all-start = ((bf16[32,2,32,128]{3,2,1,0:T(8,128)(2,1)}), bf16[32,2,32,128]{3,2,1,0:T(8,128)(2,1)S(1)}, u32[]{:S(2)}, u32[]{:S(2)}) async-start(bf16[32,2,32,128]{3,2,1,0:T(8,128)(2,1)} %copy.35), calls=%async_computation.1 | async-start | bytes 1048576 | tf_op jit(solution)/shard_map/all_to_all | solution.py:50
  271.7 244.1 %reduce-scatter.5.cloned.1.call-start = ((), (), s32[]{:S(2)}) async-start(), calls=%async_computation.6 | async-start | bytes 2228224 | tf_op jit(solution)/shard_map/reduce_scatter | solution.py:25
  417.0 2.0 copy-start.1
  425.2 90.6 %copy-start.3 = (bf16[512,512]{1,0:T(8,128)(2,1)S(1)}, bf16[512,512]{1,0:T(8,128)(2,1)}, u32[]{:S(2)}) copy-start(bf16[512,512]{1,0:T(8,128)(2,1)} %param.23) | copy-start | bytes 1572868
Sparse Core Ops, SparseCore 0:
  10.1 141.6 all-gather.2
  166.9 87.3 reduce-scatter.2
  257.1 146.4 all-gather.4
  429.2 86.5 reduce-scatter.4
where the time goes:
time: 525 us; the launch traced here: 524 us
  waiting for transfers between devices  445 us (85%)
  local copies, waits for them, and re-layouts  26.1 us (5%)
  matrix products  18.4 us (4%)
  between operations  14 us (3%)
  starting transfers between devices  13.2 us (3%)
  other arithmetic  7.57 us (1%)
    all_gather x2, waiting for transfers between devices, aggregate(): col_panel = lax.all_gather(source, 'dom', axis=0, tiled=True)  233 us
    reduce_scatter x2, waiting for transfers between devices, aggregate(): lax.psum_scatter(rounded.astype(jnp.float32).astype(jnp.bfloat16), 'grid'...  174 us
    all_to_all x1, waiting for transfers between devices, history_term(): lax.all_to_all(outgoing, 'dom', split_axis=0, concat_axis=0, tiled=True)  36.6 us
    gather x2, local copies, waits for them, and re-layouts, tile_product(): picked = jnp.take(blocks, tile_cols, axis=0)  15.4 us
    all_to_all x1, starting transfers between devices, history_term(): lax.all_to_all(outgoing, 'dom', split_axis=0, concat_axis=0, tiled=True)  13 us
    dot_general x2, matrix products, tile_product(): jnp.einsum('rkab,rkbf->raf', live_vals, picked, preferred_element_type=jn...  12.9 us
  transfers between devices with their start and end apart: 5, of which 5 were waited for; matrix products, arithmetic and copies ran while one was open for 2% of the time, Pallas kernels for 0%

commit v1 on v0

--- a/solution.py
+++ b/solution.py
@@ -7,6 +7,12 @@
 BLOCK = 128
 HOWN = 4
 CAP = 2
+change_the_desk = lambda original, shard_axis: jnp.concatenate(
+    jax.lax.all_to_all(
+        jnp.stack(jax.lax.axis_size(shard_axis) * [original], axis=0), shard_axis, 0, 0
+    ),
+    0,
+)
 
 
 def tile_product(col_panel, live_vals, tile_cols):
@@ -17,7 +23,7 @@
 
 
 def aggregate(source, live_vals, tile_cols, extra_term):
-    col_panel = lax.all_gather(source, "dom", axis=0, tiled=True)
+    col_panel = change_the_desk(source, "dom")
     partial_value = tile_product(col_panel, live_vals, tile_cols)
     if extra_term is not None:
         partial_value = partial_value + extra_term

time: 525 us -> 643 us (1.22)
  the two profiles are of different devices: /device:TPU:32 before, /device:TPU:8 now
where the time goes in v1:
time: 643 us; the launch traced here: 642 us
  waiting for transfers between devices  533 us (83%)
  starting transfers between devices  38.7 us (6%)
  local copies, waits for them, and re-layouts  32.7 us (5%)
  matrix products  17.7 us (3%)
  between operations  14.3 us (2%)
    all_to_all x2, waiting for transfers between devices, jax.lax.all_to_all(jnp.stack(jax.lax.axis_size(shard_axis) * [original],...  364 us
    reduce_scatter x2, waiting for transfers between devices, aggregate(): lax.psum_scatter(rounded.astype(jnp.float32).astype(jnp.bfloat16), 'grid'...  169 us
    all_to_all x2, starting transfers between devices, jax.lax.all_to_all(jnp.stack(jax.lax.axis_size(shard_axis) * [original],...  29.6 us
    gather x2, local copies, waits for them, and re-layouts, tile_product(): picked = jnp.take(blocks, tile_cols, axis=0)  15.4 us
    dot_general x2, matrix products, tile_product(): jnp.einsum('rkab,rkbf->raf', live_vals, picked, preferred_element_type=jn...  12.9 us
  transfers between devices with their start and end apart: 5, of which 4 were waited for; matrix products, arithmetic and copies ran while one was open for 1% of the time, Pallas kernels for 0%

profile of v1, /device:TPU:8, one launch (start us, length us, event | category | flops | bytes accessed | tf_op | source)
XLA Modules:
  0.0 642.3 jit_solution(2572543220860690685)
XLA Ops:
  7.2 0.0 copy-start
  7.2 3.4 stack.4
  10.6 0.0 copy-start.7
  10.6 0.0 copy-start.6
  10.6 0.0 copy-start.9
  10.6 16.7 %all-to-all-start = ((bf16[32,128,512]{2,1,0:T(8,128)(2,1)}), bf16[32,128,512]{2,1,0:T(8,128)(2,1)}, u32[]{:S(2)}, u32[]{:S(2)}) async-start(bf16[32,128,512]{2,1,0:T(8,128)(2,1)} %stack.4), calls=%async_computation | async-start | bytes 8388608 | tf_op jit(solution)/shard_map/all_to_all | solution.py:11
  27.3 0.0 reduce-scatter.3.cloned.1.call-start
  27.3 0.0 copy-done.7
  27.4 0.1 copy.32
  27.4 0.1 reshape.207
  27.6 0.1 copy.31
  27.6 0.0 copy-done.6
  27.7 0.0 copy-done.9
  27.7 0.1 fusion.22
  27.8 184.2 %all-to-all-done = bf16[32,128,512]{2,1,0:T(8,128)(2,1)} async-done(((bf16[32,128,512]{2,1,0:T(8,128)(2,1)}), bf16[32,128,512]{2,1,0:T(8,128)(2,1)}, u32[]{:S(2)}, u32[]{:S(2)}) %all-to-all-start) | async-done | bytes 4194336 | tf_op jit(solution)/shard_map/all_to_all | solution.py:11
  212.0 7.7 %gather_fusion.2 = bf16[64,128,512]{2,1,0:T(8,128)(2,1)} fusion(bf16[32,128,512]{2,1,0:T(8,128)(2,1)} %all-to-all-done, s32[1024]{0:T(1024)S(1)} %pad_clamp_fusion.2), kind=kCustom, calls=%fused_computation.clone | custom fusion | bytes 16777472 | tf_op jit(solution)/shard_map/jit(_take)/gather | solution.py:20
  219.7 0.0 copy-start.5
  219.7 7.2 %bitcast_convert_fusion = bf16[16,128,512]{2,1,0:T(8,128)(2,1)} fusion(bf16[16,4,128,512]{3,2,1,0:T(8,128)(2,1)} %bitcast.54, pred[16,4]{1,0:T(8,128)(4,1)S(1)} %copy.31, bf16[1,1,16,4,128,128]{5,4,3,2,1,0:T(8,128)(2,1)} %param.14, bf16[16,4]{1,0:T(8,128)(2,1)S(1)} %fusion.22), kind=kOutput, calls=%fused_computation.10 | convolution fusion | flops 1080033280 | bytes 12583104 | tf_op jit(solution)/shard_map/rkab,rkbf->raf/dot_general | solution.py:21
  226.9 0.0 copy-start.2
  226.9 0.0 reduce-scatter.3.cloned.1.call-update
  226.9 0.0 copy-done.5
  226.9 0.8 convert_reduce_fusion
  227.8 0.2 convert_reduce_fusion.1
  228.0 0.3 convolution_convert_fusion
  228.4 1.0 copy.35
  229.4 9.0 %all-to-all-start.2 = ((bf16[32,2,32,128]{3,2,1,0:T(8,128)(2,1)}), bf16[32,2,32,128]{3,2,1,0:T(8,128)(2,1)S(1)}, u32[]{:S(2)}, u32[]{:S(2)}) async-start(bf16[32,2,32,128]{3,2,1,0:T(8,128)(2,1)} %copy.35), calls=%async_computation.3 | async-start | bytes 1048576 | tf_op jit(solution)/shard_map/all_to_all | solution.py:56
  238.4 80.0 %reduce-scatter.3.cloned.1.call-done = bf16[128,512]{1,0:T(8,128)(2,1)} async-done(((bf16[2048,512]{1,0:T(8,128)(2,1)}), bf16[128,512]{1,0:T(8,128)(2,1)}) %reduce-scatter.3.cloned.1.call-update) | async-done | bytes 131088 | tf_op jit(solution)/shard_map/reduce_scatter | solution.py:31
  318.4 0.0 copy-done.2
  318.4 1.1 fusion.12
  319.6 0.0 copy-start.4
  319.6 0.0 all-to-all-done.2
  319.6 2.4 stack.5
  322.0 0.0 copy-start.10
  322.0 0.0 copy-done.4
  322.0 13.0 %all-to-all-start.1 = ((bf16[32,128,512]{2,1,0:T(8,128)(2,1)}), bf16[32,128,512]{2,1,0:T(8,128)(2,1)}, u32[]{:S(2)}, u32[]{:S(2)}) async-start(bf16[32,128,512]{2,1,0:T(8,128)(2,1)} %stack.5), calls=%async_computation.2 | async-start | bytes 8388608 | tf_op jit(solution)/shard_map/all_to_all | solution.py:11
  335.0 0.0 copy-start.8
  335.0 0.0 reduce-scatter.5.cloned.1.call-start
  335.1 0.0 copy-done.10
  335.1 0.6 gather_fusion
  335.8 0.1 broadcast_select_fusion
  335.9 0.6 gather_fusion.1
  336.5 0.0 copy-done
  336.5 0.8 fusion.10
  337.3 0.0 copy-done.8
  337.3 0.7 convolution_bitcast_fusion
  338.1 0.3 copy.41
  338.4 180.1 %all-to-all-done.1 = bf16[32,128,512]{2,1,0:T(8,128)(2,1)} async-done(((bf16[32,128,512]{2,1,0:T(8,128)(2,1)}), bf16[32,128,512]{2,1,0:T(8,128)(2,1)}, u32[]{:S(2)}, u32[]{:S(2)}) %all-to-all-start.1) | async-done | bytes 4194336 | tf_op jit(solution)/shard_map/all_to_all | solution.py:11
  518.5 7.7 %gather_fusion.3 = bf16[64,128,512]{2,1,0:T(8,128)(2,1)} fusion(bf16[32,128,512]{2,1,0:T(8,128)(2,1)} %all-to-all-done.1, s32[1024]{0:T(1024)S(1)} %pad_clamp_fusion.2), kind=kCustom, calls=%fused_computation.1.clone | custom fusion | bytes 16777472 | tf_op jit(solution)/shard_map/jit(_take)/gather | solution.py:20
  526.2 5.7 fusion
  531.9 0.0 copy-start.1
  531.9 1.9 copy-done.1
  533.9 0.4 bitcast_add_fusion
  534.3 6.6 %add.103 = f32[2048,512]{1,0:T(8,128)} dynamic-update-slice(f32[2048,512]{1,0:T(8,128)} %bitcast.56, f32[2048,32]{1,0:T(8,128)S(1)} %bitcast_add_fusion, s32[]{:T(128)} %constant.76.clone.1, s32[]{:T(128)S(6)} %select_n.66) | dynamic-update-slice | bytes 524292 | tf_op jit(solution)/shard_map/add | solution.py:29
  540.9 0.0 copy-start.3
  540.9 3.9 convert_element_type.47
  544.7 0.0 reduce-scatter.5.cloned.1.call-update
  544.7 89.0 %reduce-scatter.5.cloned.1.call-done = bf16[128,512]{1,0:T(8,128)(2,1)} async-done(((bf16[2048,512]{1,0:T(8,128)(2,1)}), bf16[128,512]{1,0:T(8,128)(2,1)}) %reduce-scatter.5.cloned.1.call-update) | async-done | bytes 131088 | tf_op jit(solution)/shard_map/reduce_scatter | solution.py:31
  633.7 0.0 copy-done.3
  633.7 1.8 convolution_convert_fusion.1
  (14 shorter events, 0.1 us)
Async XLA Ops:
  7.2 329.3 %copy-start = (bf16[1,40,128,128]{3,2,1,0:T(8,128)(2,1)S(1)}, bf16[1,40,128,128]{3,2,1,0:T(8,128)(2,1)}, u32[]{:S(2)}) copy-start(bf16[1,40,128,128]{3,2,1,0:T(8,128)(2,1)} %param.19) | copy-start | bytes 3932164
  10.6 16.7 %copy-start.7 = (s32[1,1,16,4]{2,3,1,0:T(4,128)S(1)}, s32[1,1,16,4]{2,3,1,0:T(4,128)}, u32[]{:S(2)}) copy-start(s32[1,1,16,4]{2,3,1,0:T(4,128)} %param.15) | copy-start | bytes 772
  10.6 17.0 %copy-start.6 = (bf16[32,512]{1,0:T(8,128)(2,1)S(1)}, bf16[32,512]{1,0:T(8,128)(2,1)}, u32[]{:S(2)}) copy-start(bf16[32,512]{1,0:T(8,128)(2,1)} %param.17) | copy-start | bytes 98308
  10.6 17.1 %copy-start.9 = (s32[1,1,16]{2,1,0:T(1,128)S(1)}, s32[1,1,16]{2,1,0:T(1,128)}, u32[]{:S(2)}) copy-start(s32[1,1,16]{2,1,0:T(1,128)} %param.16) | copy-start | bytes 196
  10.6 201.3 %all-to-all-start = ((bf16[32,128,512]{2,1,0:T(8,128)(2,1)}), bf16[32,128,512]{2,1,0:T(8,128)(2,1)}, u32[]{:S(2)}, u32[]{:S(2)}) async-start(bf16[32,128,512]{2,1,0:T(8,128)(2,1)} %stack.4), calls=%async_computation | async-start | bytes 8388608 | tf_op jit(solution)/shard_map/all_to_all | solution.py:11
  27.3 291.2 %reduce-scatter.3.cloned.1.call-start = ((), (), s32[]{:S(2)}) async-start(), calls=%async_computation.5 | async-start | bytes 2228224 | tf_op jit(solution)/shard_map/reduce_scatter | solution.py:31
  219.7 7.2 %copy-start.5 = (s32[32,40]{1,0:T(8,128)S(1)}, s32[32,40]{1,0:T(8,128)}, u32[]{:S(2)}) copy-start(s32[32,40]{1,0:T(8,128)} %param.18) | copy-start | bytes 15364
  226.9 91.6 %copy-start.2 = (bf16[512,512]{1,0:T(8,128)(2,1)S(1)}, bf16[512,512]{1,0:T(8,128)(2,1)}, u32[]{:S(2)}) copy-start(bf16[512,512]{1,0:T(8,128)(2,1)} %param.22) | copy-start | bytes 1572868
  229.4 90.2 %all-to-all-start.2 = ((bf16[32,2,32,128]{3,2,1,0:T(8,128)(2,1)}), bf16[32,2,32,128]{3,2,1,0:T(8,128)(2,1)S(1)}, u32[]{:S(2)}, u32[]{:S(2)}) async-start(bf16[32,2,32,128]{3,2,1,0:T(8,128)(2,1)} %copy.35), calls=%async_computation.3 | async-start | bytes 1048576 | tf_op jit(solution)/shard_map/all_to_all | solution.py:56
  319.6 2.4 copy-start.4
  322.0 13.1 %copy-start.10 = (s32[1,40]{1,0:T(1,128)S(1)}, s32[1,40]{1,0:T(1,128)}, u32[]{:S(2)}) copy-start(s32[1,40]{1,0:T(1,128)} %param.21) | copy-start | bytes 484
  322.0 196.5 %all-to-all-start.1 = ((bf16[32,128,512]{2,1,0:T(8,128)(2,1)}), bf16[32,128,512]{2,1,0:T(8,128)(2,1)}, u32[]{:S(2)}, u32[]{:S(2)}) async-start(bf16[32,128,512]{2,1,0:T(8,128)(2,1)} %stack.5), calls=%async_computation.2 | async-start | bytes 8388608 | tf_op jit(solution)/shard_map/all_to_all | solution.py:11
  335.0 2.3 copy-start.8
  335.0 298.7 %reduce-scatter.5.cloned.1.call-start = ((), (), s32[]{:S(2)}) async-start(), calls=%async_computation.6 | async-start | bytes 2228224 | tf_op jit(solution)/shard_map/reduce_scatter | solution.py:31
  531.9 1.9 copy-start.1
  540.9 92.8 %copy-start.3 = (bf16[512,512]{1,0:T(8,128)(2,1)S(1)}, bf16[512,512]{1,0:T(8,128)(2,1)}, u32[]{:S(2)}) copy-start(bf16[512,512]{1,0:T(8,128)(2,1)} %param.23) | copy-start | bytes 1572868
Sparse Core Ops, SparseCore 0:
  227.0 91.3 reduce-scatter.2
  544.9 88.7 reduce-scatter.4
